TPU v7x, 32 devices: a whole 2x2x4 slice. The times are simulated.
32 devices in a mesh: gx: 4 (over y, core), gy: 8 (over z, x).
Axes of the slice: x: 2, y: 2, z: 4, core: 2. Of those that a mesh axis runs over, the one named last changes fastest.
Arguments:
- a_blocks: bfloat16 [768, 7, 256, 256], P(('gx', 'gy'))
- prolong: bfloat16 [768, 256, 128], P(('gx', 'gy'))
- neighbour: int32 [768, 6], P(('gx', 'gy')), may hold values from 0 to 47, as said below
- ghost_send: int32 [4, 8, 8, 3], P('gx', 'gy'), may hold values from 0 to 23
- fine_agg: int32 [768], P(('gx', 'gy')), may hold values from 0 to 63, as said below
- balance: int32 [4, 8, 8], P('gx', 'gy'), may hold values from 0 to 64, as said below
- coarse_cols: int32 [256, 7], P(('gx', 'gy')), may hold values from 0 to 255, as said below
- loads: bfloat16 [256, 128, 256], P(('gx', 'gy')), may hold values from -48 to 48
Outputs:
- coarse: bfloat16 [256, 7, 128, 128], P(('gx', 'gy'))
- smoothed: bfloat16 [256, 128, 256], P(('gx', 'gy'))
Inputs may be any that keep to these rules, and one draw needn't show every extreme that they name: `neighbour`: an entry below 24 names a block row of the same device. An entry v >= 24 names slot (v - 24) % 3 of the blocks sent by the device of the same gx row at gy index (v - 24) // 3, never the device itself; every slot so named is named at least once, and the slots named from one peer are the first few of its 3; some device names all 3 slots of some peer. `fine_agg`: the owner is a device of the same gx row. Each aggregate is named by exactly three fine block rows, on three different devices. At most 3 block rows of one device name aggregates of one owner, and this is reached in every draw. Every named slot has a balance entry below 64, and some owner holds 8 aggregates. `balance`: entry 64 marks a slot that no block row names. Every coarse row of a gx row receives exactly one slot, and one owner sends at most one aggregate to each device. At most 3 block rows of one device have their target coarse row on one device, and this is reached in every draw. coarse_cols[g, 0] = g; the other entries name coarse rows of the same device or of a device whose gy index differs by one, in the same gx row.
All inputs are finite; a program needn't handle non-finite values.
Results may differ from a plain program's by a relative error of at most 0.0051.
Values may be sent and summed in bfloat16 or wider, within the bound.
No kernel may reach another device: no remote copies, remote signals or barrier semaphores. Data moves between devices by JAX's collectives and lax.ppermute only.
A program may use at most 128 MiB of HBM per device.

v0:
```python
import jax
import jax.numpy as jnp
from jax import lax
from jax.sharding import PartitionSpec as P

OCAP = 3
SWEEPS = 2


def padded_2(block, sides, width):
    for axis, dim in sides:
        count = lax.axis_size(axis)
        forward = [(i, i + 1) for i in range(count - 1)]
        backward = [(target, source) for source, target in forward]
        low = lax.ppermute(
            lax.slice_in_dim(block, block.shape[dim] - width, None, axis=dim), axis, forward
        )
        high = lax.ppermute(lax.slice_in_dim(block, 0, width, axis=dim), axis, backward)
        block = jnp.concatenate([low, block, high], axis=dim)
    return block


def rank_within(labels, label_count):
    one_hot = (labels[:, None] == jnp.arange(label_count, dtype=jnp.int32)[None, :]).astype(
        jnp.int32
    )
    running = jnp.cumsum(one_hot, axis=0) - one_hot
    return jnp.sum(running * one_hot, axis=1)


def place_rows(values, tag_values, positions, capacity, empty_tag):
    buffer = (
        jnp.zeros((capacity,) + values.shape[1:], values.dtype)
        .at[positions]
        .set(values, mode="drop")
    )
    labels = jnp.full((capacity,), empty_tag, jnp.int32).at[positions].set(tag_values, mode="drop")
    return (buffer, labels)


def sum_tagged(values, labels, label_count):
    selector = (jnp.arange(label_count, dtype=jnp.int32)[:, None] == labels[None, :]).astype(
        values.dtype
    )
    return jnp.einsum("ts,skab->tkab", selector, values, preferred_element_type=jnp.float32)


def per_device(a_blocks, prolong, neighbour, ghost_send, fine_agg, balance, coarse_cols, loads):
    block_rows = a_blocks.shape[0]
    group_size = lax.axis_size("gy")
    row_gy = lax.axis_index("gy")
    row_gx = lax.axis_index("gx")
    ghost_cap = ghost_send.shape[3]
    outgoing = prolong[ghost_send[0, 0]]
    arrived = lax.all_to_all(outgoing, "gy", split_axis=0, concat_axis=0, tiled=True)
    block_pool = jnp.concatenate(
        [prolong, arrived.reshape((group_size * ghost_cap,) + prolong.shape[1:])], axis=0
    )
    self_index = jnp.arange(block_rows, dtype=jnp.int32)[:, None]
    columns = jnp.concatenate([self_index, neighbour], axis=1)
    right_blocks = block_pool[columns]
    applied = jnp.einsum(
        "ikab,ikbc->ikac", a_blocks, right_blocks, preferred_element_type=jnp.float32
    ).astype(jnp.bfloat16)
    partial_value = jnp.einsum(
        "iac,ikad->ikcd", prolong, applied, preferred_element_type=jnp.float32
    ).astype(jnp.bfloat16)
    slot_count = balance.shape[2]
    coarse_rows = loads.shape[0]
    owner_dev = fine_agg // slot_count
    slot_index = fine_agg % slot_count
    placing = owner_dev * OCAP + rank_within(owner_dev, group_size)
    buffer, labels = place_rows(partial_value, slot_index, placing, group_size * OCAP, slot_count)
    received, received_labels = (
        lax.all_to_all(buffer, "gy", split_axis=0, concat_axis=0, tiled=True),
        lax.all_to_all(labels, "gy", split_axis=0, concat_axis=0, tiled=True),
    )
    held_rows = sum_tagged(received, received_labels, slot_count).astype(jnp.bfloat16)
    destination = balance[0, 0]
    peer_index = destination // coarse_rows
    within = destination % coarse_rows
    moving, moving_labels = place_rows(held_rows, within, peer_index, group_size, coarse_rows)
    arrived_rows, arrived_labels = (
        lax.all_to_all(moving, "gy", split_axis=0, concat_axis=0, tiled=True),
        lax.all_to_all(moving_labels, "gy", split_axis=0, concat_axis=0, tiled=True),
    )
    coarse = sum_tagged(arrived_rows, arrived_labels, coarse_rows).astype(jnp.bfloat16)
    magnitude = jnp.sum(jnp.abs(coarse.astype(jnp.float32)), axis=(1, 3))
    largest = lax.pmax(jnp.max(magnitude), ("gx", "gy"))
    lower_end = largest / 30.0
    centre = (largest + lower_end) / 2.0
    half_width = (largest - lower_end) / 2.0
    sigma_ratio = centre / half_width
    right_side = loads.astype(jnp.float32)
    solution = right_side / centre
    update = solution
    weight_now = 1.0 / sigma_ratio
    first_col = (row_gx * group_size + row_gy - 1) * coarse_rows
    local_cols = coarse_cols - first_col
    for sweep_index in range(SWEEPS):
        rounded = solution.astype(jnp.bfloat16)
        padded = padded_2(rounded, (("gy", 0),), coarse_rows)
        picked = padded[local_cols]
        product = jnp.einsum("rkab,rkbl->ral", coarse, picked, preferred_element_type=jnp.float32)
        residual = right_side - product
        weight_next = 1.0 / (2.0 * sigma_ratio - weight_now)
        update = weight_next * weight_now * update + 2.0 * weight_next / half_width * residual
        solution = solution + update
        weight_now = weight_next
    return (coarse, solution.astype(jnp.bfloat16))


def solution(mesh):
    return jax.shard_map(
        per_device,
        mesh=mesh,
        in_specs=(
            P(("gx", "gy"), None, None, None),
            P(("gx", "gy"), None, None),
            P(("gx", "gy"), None),
            P("gx", "gy", None, None),
            P(("gx", "gy")),
            P("gx", "gy", None),
            P(("gx", "gy"), None),
            P(("gx", "gy"), None, None),
        ),
        out_specs=(P(("gx", "gy"), None, None, None), P(("gx", "gy"), None, None)),
        check_vma=False,
    )
```

profile of v0, /device:TPU:17, one launch (start us, length us, event | category | flops | bytes accessed | tf_op | source)
XLA Modules:
  0.0 415.0 jit_solution(4881568314107393214)
XLA Ops:
  0.6 0.7 compare_select_fusion.2
  1.5 3.4 gather_fusion
  4.9 5.6 %all-to-all-start.2 = ((bf16[8,3,256,128]{3,2,1,0:T(8,128)(2,1)}), bf16[8,3,256,128]{3,2,1,0:T(8,128)(2,1)S(1)}, u32[]{:S(2)}, u32[]{:S(2)}) async-start(bf16[8,3,256,128]{3,2,1,0:T(8,128)(2,1)} %bitcast.10), calls=%async_computation.2 | async-start | bytes 3145728 | tf_op jit(solution)/shard_map/all_to_all | solution.py:55
  10.6 0.2 select_reduce_fusion
  10.8 0.7 scatter_custom_fusion.1
  11.4 0.7 all_to_all.23
  12.2 0.1 reshape.199
  12.3 31.3 %all-to-all-done.2 = bf16[8,3,256,128]{3,2,1,0:T(8,128)(2,1)S(1)} async-done(((bf16[8,3,256,128]{3,2,1,0:T(8,128)(2,1)}), bf16[8,3,256,128]{3,2,1,0:T(8,128)(2,1)S(1)}, u32[]{:S(2)}, u32[]{:S(2)}) %all-to-all-start.2) | async-done | bytes 1572896 | tf_op jit(solution)/shard_map/all_to_all | solution.py:55
  43.7 7.6 %all-to-all-start.1 = ((s32[8,3,1]{1,2,0:T(1,128)}), s32[8,3,1]{1,2,0:T(1,128)S(1)}, u32[]{:S(2)}, u32[]{:S(2)}) async-start(s32[8,3,1]{1,2,0:T(1,128)} %bitcast.6), calls=%async_computation.1 | async-start | bytes 8192 | tf_op jit(solution)/shard_map/all_to_all | solution.py:76
  51.3 2.2 pad_maximum_fusion
  53.4 7.8 %gather_fusion.1 = bf16[168,256,128]{2,1,0:T(8,128)(2,1)} fusion(bf16[48,256,128]{2,1,0:T(8,128)(2,1)S(1)} %pad_maximum_fusion, s32[1024]{0:T(1024)S(1)} %pad_clamp_fusion.1), kind=kCustom, calls=%fused_computation.1 | custom fusion | bytes 22020768 | tf_op jit(solution)/shard_map/gather | solution.py:61
  61.2 19.0 %convert_bitcast_fusion = bf16[24,7,128,128]{2,3,1,0:T(8,128)(2,1)} fusion(bf16[24,7,256,128]{3,2,1,0:T(8,128)(2,1)} %bitcast.77, bf16[24,7,256,256]{3,2,1,0:T(8,128)(2,1)} %param.8, bf16[24,256,128]{2,1,0:T(8,128)(2,1)} %param.9), kind=kOutput, calls=%fused_computation.14 | convolution fusion | flops 4236115968 | bytes 40108032 | tf_op jit(solution)/shard_map/iac,ikad->ikcd/dot_general | solution.py:65
  80.2 8.3 %copy.49 = bf16[24,7,128,128]{3,2,1,0:T(8,128)(2,1)} copy(bf16[24,7,128,128]{2,3,1,0:T(8,128)(2,1)} %convert_bitcast_fusion) | data formatting | bytes 11010048 | tf_op jit(solution)/shard_map/convert_element_type | solution.py:67
  88.5 3.8 broadcast_in_dim.10
  92.4 16.3 %scatter_fusion = bf16[24,7,128,128]{3,2,1,0:T(8,128)(2,1)} fusion(bf16[24,7,128,128]{3,2,1,0:T(8,128)(2,1)} %broadcast_in_dim.10, s32[24]{0:T(128)S(1)} %compare_select_fusion.3, bf16[24,7,128,128]{3,2,1,0:T(8,128)(2,1)} %copy.49), kind=kCustom, calls=%fused_computation.6 | custom fusion | bytes 16515168 | tf_op jit(solution)/shard_map/scatter | solution.py:35
  108.6 5.5 %all-to-all-start.3 = ((bf16[24,7,128,128]{3,2,1,0:T(8,128)(2,1)}), bf16[24,7,128,128]{3,2,1,0:T(8,128)(2,1)}, u32[]{:S(2)}, u32[]{:S(2)}) async-start(bf16[24,7,128,128]{3,2,1,0:T(8,128)(2,1)} %scatter_fusion), calls=%async_computation.3 | async-start | bytes 11010048 | tf_op jit(solution)/shard_map/all_to_all | solution.py:75
  114.2 0.6 scatter_custom_fusion
  114.8 0.7 copy.44
  115.5 0.5 broadcast.213
  116.0 0.7 reduce.4
  116.7 114.5 %all-to-all-done.3 = bf16[24,7,128,128]{3,2,1,0:T(8,128)(2,1)} async-done(((bf16[24,7,128,128]{3,2,1,0:T(8,128)(2,1)}), bf16[24,7,128,128]{3,2,1,0:T(8,128)(2,1)}, u32[]{:S(2)}, u32[]{:S(2)}) %all-to-all-start.3) | async-done | bytes 5505056 | tf_op jit(solution)/shard_map/all_to_all | solution.py:75
  231.3 8.1 %all-to-all-start = ((s32[8,1,1]{2,1,0:T(1,128)}), s32[8,1,1]{2,1,0:T(1,128)S(1)}, u32[]{:S(2)}, u32[]{:S(2)}) async-start(s32[8,1,1]{2,1,0:T(1,128)} %copy.44), calls=%async_computation | async-start | bytes 8192 | tf_op jit(solution)/shard_map/all_to_all | solution.py:85
  239.4 6.5 %fusion.14 = bf16[8,7,128,128]{3,0,2,1:T(8,128)(2,1)S(1)} fusion(bf16[24,7,128,128]{3,2,1,0:T(8,128)(2,1)} %all-to-all-done.3, s32[24]{0:T(128)S(1)} %eq.55), kind=kOutput, calls=%fused_computation.20 | convolution fusion | flops 44957888 | bytes 7340128 | tf_op jit(solution)/shard_map/ts,skab->tkab/dot_general | solution.py:45
  245.9 0.5 copy.51
  246.3 1.7 broadcast_in_dim.8
  248.0 5.0 %scatter_fusion.1 = bf16[8,7,128,128]{3,2,1,0:T(8,128)(2,1)} fusion(bf16[8,7,128,128]{3,2,1,0:T(8,128)(2,1)} %broadcast_in_dim.8, s32[8]{0:T(128)S(1)} %fusion.32, bf16[8,7,128,128]{3,2,1,0:T(8,128)(2,1)S(1)} %copy.51), kind=kCustom, calls=%fused_computation.7 | custom fusion | bytes 5505056 | tf_op jit(solution)/shard_map/scatter | solution.py:35
  253.0 5.6 %all-to-all-start.4 = ((bf16[8,7,128,128]{3,2,1,0:T(8,128)(2,1)}), bf16[8,7,128,128]{3,2,1,0:T(8,128)(2,1)S(1)}, u32[]{:S(2)}, u32[]{:S(2)}) async-start(bf16[8,7,128,128]{3,2,1,0:T(8,128)(2,1)} %scatter_fusion.1), calls=%async_computation.4 | async-start | bytes 3670016 | tf_op jit(solution)/shard_map/all_to_all | solution.py:84
  258.6 0.2 reduce
  258.9 38.2 %all-to-all-done.4 = bf16[8,7,128,128]{3,2,1,0:T(8,128)(2,1)S(1)} async-done(((bf16[8,7,128,128]{3,2,1,0:T(8,128)(2,1)}), bf16[8,7,128,128]{3,2,1,0:T(8,128)(2,1)S(1)}, u32[]{:S(2)}, u32[]{:S(2)}) %all-to-all-start.4) | async-done | bytes 1835040 | tf_op jit(solution)/shard_map/all_to_all | solution.py:84
  297.1 2.8 abs_reduce_fusion
  299.8 0.6 reduce_max.9
  300.5 42.1 %pmax.7 = f32[]{:T(128)} all-reduce(f32[]{:T(128)} %reduce_max.9), channel_id=1, replica_groups=mesh['gx'=4,'gy'=8] {'gx','gy'}, use_global_device_ids=true, to_apply=%region_8.9 | all-reduce | flops 1 | bytes 8 | tf_op jit(solution)/shard_map/pmax | solution.py:89
  343.9 3.4 collective-permute-start
  347.3 2.8 collective-permute-start.1
  351.1 3.2 copy.55
  354.3 13.7 %collective-permute-done = bf16[8,128,256]{2,1,0:T(8,128)(2,1)S(1)} collective-permute-done((bf16[8,128,256]{2,1,0:T(8,128)(2,1)S(1)}, bf16[8,128,256]{2,1,0:T(8,128)(2,1)S(1)}, u32[]{:S(2)}, u32[]{:S(2)}) %collective-permute-start) | collective-permute-done | bytes 524320 | tf_op jit(solution)/shard_map/ppermute | solution.py:15
  368.0 3.8 collective-permute-done.1
  371.8 0.2 pad_maximum_fusion.1
  372.0 2.6 gather_fusion.2
  374.6 4.0 fusion.23
  378.7 1.9 collective-permute-start.2
  380.6 4.3 %collective-permute-start.3 = (bf16[8,128,256]{2,1,0:T(8,128)(2,1)S(1)}, bf16[8,128,256]{2,1,0:T(8,128)(2,1)}, u32[]{:S(2)}, u32[]{:S(2)}) collective-permute-start(bf16[8,128,256]{2,1,0:T(8,128)(2,1)S(1)} %get-tuple-element.16), channel_id=1, source_target_pairs={{1,0},{2,1},{3,2},{4,3},{5,4},{6,5},{7,6},{9,8},{10,9},{11,10},{12... | collective-permute-start | bytes 1572872 | tf_op jit(solution)/shard_map/ppermute | solution.py:18
  385.0 17.1 %collective-permute-done.2 = bf16[8,128,256]{2,1,0:T(8,128)(2,1)S(1)} collective-permute-done((bf16[8,128,256]{2,1,0:T(8,128)(2,1)S(1)}, bf16[8,128,256]{2,1,0:T(8,128)(2,1)S(1)}, u32[]{:S(2)}, u32[]{:S(2)}) %collective-permute-start.2) | collective-permute-done | bytes 524320 | tf_op jit(solution)/shard_map/ppermute | solution.py:15
  402.0 0.8 copy-done.4
  402.9 3.8 collective-permute-done.3
  406.6 1.5 pad_maximum_fusion.2
  408.2 2.6 gather_fusion.3
  410.8 4.2 %add_convert_fusion = bf16[8,128,256]{2,1,0:T(8,128)(2,1)} fusion(f32[8,128,256]{2,1,0:T(8,128)} %get-tuple-element.17, bf16[8,7,128,128]{3,2,1,0:T(8,128)(2,1)S(1)} %copy-done.1, bf16[8,7,128,256]{3,2,1,0:T(8,128)(2,1)} %bitcast.79, bf16[8,128,256]{2,1,0:T(8,128)(2,1)} %param.15, f32[]{:T(128)S(6)} %div.75, f32[]{:T(128)S(6)} %mul.63, f32[]{:T(128)S(6)} %div.66), kind=kOutput, calls=%fused_computation.32 | convolution fusion | flops 472121344 | bytes 7602188 | tf_op jit(solution)/shard_map/rkab,rkbl->ral/dot_general | solution.py:104
  (37 shorter events, 0.7 us)
Async XLA Ops:
  1.5 9.0 %copy-start.7 = (s32[24]{0:T(128)S(1)}, s32[24]{0:T(128)}, u32[]{:S(2)}) copy-start(s32[24]{0:T(128)} %param.12) | copy-start | bytes 292
  1.5 10.6 %copy-start.5 = (s32[24,6]{0,1:T(8,128)S(1)}, s32[24,6]{0,1:T(8,128)}, u32[]{:S(2)}) copy-start(s32[24,6]{0,1:T(8,128)} %param.10) | copy-start | bytes 1732
  4.9 38.8 %all-to-all-start.2 = ((bf16[8,3,256,128]{3,2,1,0:T(8,128)(2,1)}), bf16[8,3,256,128]{3,2,1,0:T(8,128)(2,1)S(1)}, u32[]{:S(2)}, u32[]{:S(2)}) async-start(bf16[8,3,256,128]{3,2,1,0:T(8,128)(2,1)} %bitcast.10), calls=%async_computation.2 | async-start | bytes 3145728 | tf_op jit(solution)/shard_map/all_to_all | solution.py:55
  43.7 7.6 %copy-start = (bf16[8,3,256,128]{3,2,1,0:T(8,128)(2,1)}, bf16[8,3,256,128]{3,2,1,0:T(8,128)(2,1)S(1)}, u32[]{:S(2)}) copy-start(bf16[8,3,256,128]{3,2,1,0:T(8,128)(2,1)S(1)} %all-to-all-done.2) | copy-start | bytes 4718596
  43.7 65.0 %all-to-all-start.1 = ((s32[8,3,1]{1,2,0:T(1,128)}), s32[8,3,1]{1,2,0:T(1,128)S(1)}, u32[]{:S(2)}, u32[]{:S(2)}) async-start(s32[8,3,1]{1,2,0:T(1,128)} %bitcast.6), calls=%async_computation.1 | async-start | bytes 8192 | tf_op jit(solution)/shard_map/all_to_all | solution.py:76
  108.6 5.6 %copy-start.8 = (s32[1,1,8]{2,1,0:T(1,128)S(1)}, s32[1,1,8]{2,1,0:T(1,128)}, u32[]{:S(2)}) copy-start(s32[1,1,8]{2,1,0:T(1,128)} %param.13) | copy-start | bytes 100
  108.6 122.7 %all-to-all-start.3 = ((bf16[24,7,128,128]{3,2,1,0:T(8,128)(2,1)}), bf16[24,7,128,128]{3,2,1,0:T(8,128)(2,1)}, u32[]{:S(2)}, u32[]{:S(2)}) async-start(bf16[24,7,128,128]{3,2,1,0:T(8,128)(2,1)} %scatter_fusion), calls=%async_computation.3 | async-start | bytes 11010048 | tf_op jit(solution)/shard_map/all_to_all | solution.py:75
  231.3 21.8 %all-to-all-start = ((s32[8,1,1]{2,1,0:T(1,128)}), s32[8,1,1]{2,1,0:T(1,128)S(1)}, u32[]{:S(2)}, u32[]{:S(2)}) async-start(s32[8,1,1]{2,1,0:T(1,128)} %copy.44), calls=%async_computation | async-start | bytes 8192 | tf_op jit(solution)/shard_map/all_to_all | solution.py:85
  253.0 90.8 %copy-start.2 = (bf16[8,128,256]{2,1,0:T(8,128)(2,1)S(1)}, bf16[8,128,256]{2,1,0:T(8,128)(2,1)}, u32[]{:S(2)}) copy-start(bf16[8,128,256]{2,1,0:T(8,128)(2,1)} %param.15) | copy-start | bytes 1572868
  253.0 44.0 %all-to-all-start.4 = ((bf16[8,7,128,128]{3,2,1,0:T(8,128)(2,1)}), bf16[8,7,128,128]{3,2,1,0:T(8,128)(2,1)S(1)}, u32[]{:S(2)}, u32[]{:S(2)}) async-start(bf16[8,7,128,128]{3,2,1,0:T(8,128)(2,1)} %scatter_fusion.1), calls=%async_computation.4 | async-start | bytes 3670016 | tf_op jit(solution)/shard_map/all_to_all | solution.py:84
  258.6 91.5 %copy-start.6 = (s32[8,7]{1,0:T(8,128)S(1)}, s32[8,7]{1,0:T(8,128)}, u32[]{:S(2)}) copy-start(s32[8,7]{1,0:T(8,128)} %param.14) | copy-start | bytes 676
  343.9 24.0 %collective-permute-start = (bf16[8,128,256]{2,1,0:T(8,128)(2,1)S(1)}, bf16[8,128,256]{2,1,0:T(8,128)(2,1)S(1)}, u32[]{:S(2)}, u32[]{:S(2)}) collective-permute-start(bf16[8,128,256]{2,1,0:T(8,128)(2,1)S(1)} %fusion.22), channel_id=1, source_target_pairs={{0,1},{1,2},{2,3},{3,4},{4,5},{5,6},{6,7},{8,9},{9,10},{10,11},{11... | collective-permute-start | bytes 1572872 | tf_op jit(solution)/shard_map/ppermute | solution.py:15
  347.3 24.5 %collective-permute-start.1 = (bf16[8,128,256]{2,1,0:T(8,128)(2,1)S(1)}, bf16[8,128,256]{2,1,0:T(8,128)(2,1)S(1)}, u32[]{:S(2)}, u32[]{:S(2)}) collective-permute-start(bf16[8,128,256]{2,1,0:T(8,128)(2,1)S(1)} %fusion.22), channel_id=1, source_target_pairs={{1,0},{2,1},{3,2},{4,3},{5,4},{6,5},{7,6},{9,8},{10,9},{11,10},{12... | collective-permute-start | bytes 1572872 | tf_op jit(solution)/shard_map/ppermute | solution.py:18
  372.0 2.6 copy-start.1
  378.7 23.4 %copy-start.3 = (bf16[8,128,256]{2,1,0:T(8,128)(2,1)}, bf16[8,128,256]{2,1,0:T(8,128)(2,1)S(1)}, u32[]{:S(2)}) copy-start(bf16[8,128,256]{2,1,0:T(8,128)(2,1)S(1)} %get-tuple-element.16) | copy-start | bytes 1572868
  378.7 23.4 %collective-permute-start.2 = (bf16[8,128,256]{2,1,0:T(8,128)(2,1)S(1)}, bf16[8,128,256]{2,1,0:T(8,128)(2,1)S(1)}, u32[]{:S(2)}, u32[]{:S(2)}) collective-permute-start(bf16[8,128,256]{2,1,0:T(8,128)(2,1)S(1)} %get-tuple-element.16), channel_id=1, source_target_pairs={{0,1},{1,2},{2,3},{3,4},{4,5},{5,6},{6,7},{8,9},{9,10},{10,11},{11... | collective-permute-start | bytes 1572872 | tf_op jit(solution)/shard_map/ppermute | solution.py:15
  380.6 26.1 %collective-permute-start.3 = (bf16[8,128,256]{2,1,0:T(8,128)(2,1)S(1)}, bf16[8,128,256]{2,1,0:T(8,128)(2,1)}, u32[]{:S(2)}, u32[]{:S(2)}) collective-permute-start(bf16[8,128,256]{2,1,0:T(8,128)(2,1)S(1)} %get-tuple-element.16), channel_id=1, source_target_pairs={{1,0},{2,1},{3,2},{4,3},{5,4},{6,5},{7,6},{9,8},{10,9},{11,10},{12... | collective-permute-start | bytes 1572872 | tf_op jit(solution)/shard_map/ppermute | solution.py:18
  402.0 0.8 copy-start.4
where the time goes:
time: 417 us; the launch traced here: 415 us
  waiting for transfers between devices  222 us (53%)
  local copies, waits for them, and re-layouts  59.6 us (14%)
  starting transfers between devices  44.8 us (11%)
  blocking collectives  42.1 us (10%)
  matrix products  36.5 us (9%)
  other arithmetic  6.52 us (2%)
    all_to_all x1, waiting for transfers between devices, per_device(): lax.all_to_all(buffer, 'gy', split_axis=0, concat_axis=0, tiled=True)  115 us
    pmax x1, blocking collectives, per_device(): largest = lax.pmax(jnp.max(magnitude), ('gx', 'gy'))  42.1 us
    all_to_all x1, waiting for transfers between devices, per_device(): lax.all_to_all(moving, 'gy', split_axis=0, concat_axis=0, tiled=True)  38.2 us
    all_to_all x1, waiting for transfers between devices, per_device(): lax.all_to_all(outgoing, 'gy', split_axis=0, concat_axis=0, tiled=True)  31.3 us
    ppermute x2, waiting for transfers between devices, padded_2(): lax.ppermute(lax.slice_in_dim(block, block.shape[dim] - width, None, axis...  30.8 us
    scatter x2, local copies, waits for them, and re-layouts, place_rows(): buffer = jnp.zeros((capacity,) + values.shape[1:], values.dtype).at[posit...  21.3 us
    dot_general x1, matrix products, per_device(): jnp.einsum('iac,ikad->ikcd', prolong, applied, preferred_element_type=jnp...  19 us
    dot_general x2, matrix products, sum_tagged(): jnp.einsum('ts,skab->tkab', selector, values, preferred_element_type=jnp....  9.26 us
  transfers between devices with their start and end apart: 9, of which 7 were waited for; matrix products, arithmetic and copies ran while one was open for 19% of the time, Pallas kernels for 0%

commit v1 on v0

v1 whole, which is shorter than its diff:
```python
import functools

import jax
import jax.numpy as jnp
from jax import lax
from jax.experimental import pallas as pl
from jax.experimental.pallas import tpu as pltpu
from jax.sharding import PartitionSpec as P

OCAP = 3
MEMBERS = 3
CHUNKS = 3

F32 = jnp.float32
BF16 = jnp.bfloat16
VMEM = pltpu.VMEM
ANY = pl.ANY


def chunks_of(count):
    rest = list(range(1, count))
    parts = CHUNKS - 1
    size = -(-len(rest) // parts)
    return [(0, 1)] + [
        (rest[at], min(size, len(rest) - at)) for at in range(0, len(rest), size)
    ]


def dot(a, b):
    return lax.dot_general(a, b, (((1,), (0,)), ((), ())), preferred_element_type=F32)


def dot_t(a, b):
    return lax.dot_general(a, b, (((0,), (0,)), ((), ())), preferred_element_type=F32)


def galerkin_kernel(first, count, per_step, block_rows, ghosts, order, cols, *refs):
    blocks = refs[: per_step * count]
    prolong = refs[per_step * count]
    arrived = refs[per_step * count + 1] if ghosts else None
    out = refs[-1]
    step = pl.program_id(0)
    for s in range(per_step):
        row = order[step * per_step + s]
        left = prolong[row]
        applied = []
        for k in range(count):
            if first + k == 0:
                right = left
            else:
                col = cols[row, first + k]
                near = prolong[jnp.minimum(col, block_rows - 1)]
                far = arrived[jnp.clip(col - block_rows, 0, ghosts - 1)]
                right = jnp.where(col < block_rows, near, far)
            applied.append(dot(blocks[s * count + k][...], right).astype(BF16))
        width = applied[0].shape[1]
        for k in range(0, count, 2):
            if k + 1 < count:
                both = dot_t(left, jnp.concatenate(applied[k : k + 2], axis=1)).astype(BF16)
                out[s, k] = both[:, :width]
                out[s, k + 1] = both[:, width:]
            else:
                out[s, k] = dot_t(left, applied[k]).astype(BF16)


def galerkin(a_blocks, prolong, arrived, order, cols, first, count):
    rows, _, size, _ = a_blocks.shape
    width = prolong.shape[2]
    slots = order.shape[0]
    per_step = OCAP

    def block_spec(s, k):
        return pl.BlockSpec(
            (None, None, size, size),
            lambda step, order, cols: (order[step * per_step + s], k, 0, 0),
        )

    def whole(array):
        return pl.BlockSpec(array.shape, lambda step, order, cols: (0,) * array.ndim)

    ghosts = 0 if arrived is None else arrived.shape[0]
    pools = [prolong] if arrived is None else [prolong, arrived]
    specs = [block_spec(s, first + k) for s in range(per_step) for k in range(count)]
    return pl.pallas_call(
        functools.partial(galerkin_kernel, first, count, per_step, rows, ghosts),
        out_shape=jax.ShapeDtypeStruct((slots, count, width, width), BF16),
        grid_spec=pltpu.PrefetchScalarGridSpec(
            num_scalar_prefetch=2,
            grid=(slots // per_step,),
            in_specs=specs + [whole(array) for array in pools],
            out_specs=pl.BlockSpec(
                (per_step, count, width, width), lambda step, order, cols: (step, 0, 0, 0)
            ),
        ),
        cost_estimate=pl.CostEstimate(
            flops=2 * slots * count * (size * size * width + size * width * width),
            bytes_accessed=2 * slots * count * (size * size + width * width),
            transcendentals=0,
        ),
        name=f"galerkin_{first}",
    )(order, cols, *([a_blocks] * len(specs)), *pools)


def member_sum(members, recv, row, k):
    total = recv[members[row, 0], k].astype(F32)
    for m in range(1, MEMBERS):
        total = total + recv[members[row, m], k].astype(F32)
    return total.astype(BF16)


def gather_kernel(first, count, members, recv, *refs):
    out, held, sem = refs[-3:]
    rows = held.shape[0]

    def one(row, carry):
        for k in range(count):
            held[row, k] = member_sum(members, recv, row, k)
        return carry

    lax.fori_loop(0, rows, one, 0)
    copy = pltpu.make_async_copy(held, out.at[:, pl.ds(first, count)], sem)
    copy.start()
    copy.wait()


def gather_rows(members, recv, so_far, shape, first, count):
    rows, _, width, _ = shape
    inputs = [recv] if so_far is None else [recv, so_far]
    return pl.pallas_call(
        functools.partial(gather_kernel, first, count),
        out_shape=jax.ShapeDtypeStruct(shape, BF16),
        grid_spec=pltpu.PrefetchScalarGridSpec(
            num_scalar_prefetch=1,
            in_specs=[pl.BlockSpec(memory_space=VMEM)]
            + ([] if so_far is None else [pl.BlockSpec(memory_space=ANY)]),
            out_specs=pl.BlockSpec(memory_space=ANY),
            scratch_shapes=[VMEM((rows, count, width, width), BF16), pltpu.SemaphoreType.DMA],
        ),
        input_output_aliases={} if so_far is None else {2: 0},
        cost_estimate=pl.CostEstimate(
            flops=2 * recv.size, bytes_accessed=3 * recv.size, transcendentals=0
        ),
        name=f"gather_{first}",
    )(members, *inputs)


def block_row_product(coarse, pool, cols, row, count):
    total = None
    for k in range(0, count, 2):
        if k + 1 < count:
            lhs = jnp.concatenate([coarse[row, k], coarse[row, k + 1]], axis=1)
            rhs = jnp.concatenate([pool[cols[row, k]], pool[cols[row, k + 1]]], axis=0)
        else:
            lhs, rhs = coarse[row, k], pool[cols[row, k]]
        term = dot(lhs, rhs)
        total = term if total is None else total + term
    return total


def first_kernel(
    first, count, blocks, members, cols, recv, so_far, low, own, high,
    out, product, sent, peak, held, pool, row_sums, sem_in, sem_out,
):
    rows = product.shape[0]
    load = pltpu.make_async_copy(so_far.at[:, pl.ds(0, first)], held.at[:, pl.ds(0, first)], sem_in)
    load.start()

    def last(row, carry):
        for k in range(count):
            held[row, first + k] = member_sum(members, recv, row, k)
        return carry

    lax.fori_loop(0, rows, last, 0)
    store = pltpu.make_async_copy(
        held.at[:, pl.ds(first, count)], out.at[:, pl.ds(first, count)], sem_out
    )
    store.start()
    load.wait()

    def sums(row, carry):
        total = jnp.abs(held[row, 0].astype(F32))
        for k in range(1, blocks):
            total = total + jnp.abs(held[row, k].astype(F32))
        return jnp.maximum(carry, jnp.sum(total, axis=1, keepdims=True))

    width = held.shape[2]
    most = lax.fori_loop(0, rows, sums, jnp.zeros((width, 1), F32))
    most = jnp.max(most, axis=0, keepdims=True)
    peak[...] = jnp.broadcast_to(most[None], peak.shape)
    scale = 1.0 / jnp.clip(most, 2.0**-100, 2.0**120)
    for part, source in enumerate((low, own, high)):

        def scaled(row, carry):
            pool[part * rows + row] = (source[row].astype(F32) * scale).astype(BF16)
            return carry

        lax.fori_loop(0, rows, scaled, 0)

    def multiply(row, carry):
        total = block_row_product(held, pool, cols, row, blocks)
        product[row] = total
        sent[row] = total.astype(BF16)
        return carry

    lax.fori_loop(0, rows, multiply, 0)
    store.wait()


def first_product(members, cols, recv, so_far, low, own, high, first, count, devices):
    rows, blocks, width, _ = so_far.shape
    columns = own.shape[2]
    vmem = pl.BlockSpec(memory_space=VMEM)
    hbm = pl.BlockSpec(memory_space=ANY)
    return pl.pallas_call(
        functools.partial(first_kernel, first, count, blocks),
        out_shape=(
            jax.ShapeDtypeStruct(so_far.shape, BF16),
            jax.ShapeDtypeStruct(own.shape, F32),
            jax.ShapeDtypeStruct(own.shape, BF16),
            jax.ShapeDtypeStruct((devices, 8, 128), F32),
        ),
        grid_spec=pltpu.PrefetchScalarGridSpec(
            num_scalar_prefetch=2,
            in_specs=[vmem, hbm, vmem, vmem, vmem],
            out_specs=(hbm, vmem, vmem, vmem),
            scratch_shapes=[
                VMEM(so_far.shape, BF16),
                VMEM((3 * rows, width, columns), BF16),
                VMEM((8, 128), F32),
                pltpu.SemaphoreType.DMA,
                pltpu.SemaphoreType.DMA,
            ],
        ),
        input_output_aliases={3: 0},
        cost_estimate=pl.CostEstimate(
            flops=2 * so_far.size * columns, bytes_accessed=6 * so_far.size, transcendentals=0
        ),
        name="first_product",
    )(members, cols, recv, so_far, low, own, high)


def second_kernel(blocks, cols, near, coarse, low, own, high, product, below, above, peaks, out, pool):
    rows = out.shape[0]
    largest = jnp.max(jnp.max(peaks[...], axis=0)[0:1], axis=1, keepdims=True)
    lower_end = largest / 30.0
    centre = (largest + lower_end) / 2.0
    half_width = (largest - lower_end) / 2.0
    sigma = centre / half_width
    weight_0 = 1.0 / sigma
    weight_1 = 1.0 / (2.0 * sigma - weight_0)
    weight_2 = 1.0 / (2.0 * sigma - weight_1)
    start = 1.0 / centre
    gain_1 = 2.0 * weight_1 / half_width
    gain_2 = 2.0 * weight_2 / half_width
    change = weight_1 * weight_0 * start + gain_1

    def back(slot):
        peak = peaks[near[slot]][0:1, 0:1]
        return gain_1 * (jnp.clip(peak, 2.0**-100, 2.0**120) / centre)

    for part, (source, seen) in enumerate(((low, below), (own, product), (high, above))):
        factor = back(part)

        def iterate(row, carry):
            value = (start + change) * source[row].astype(F32) - factor * seen[row].astype(F32)
            pool[part * rows + row] = value.astype(BF16)
            return carry

        lax.fori_loop(0, rows, iterate, 0)
    mine = back(1)

    def multiply(row, carry):
        right = own[row].astype(F32)
        update = change * right - mine * product[row]
        residual = right - block_row_product(coarse, pool, cols, row, blocks)
        value = start * right + update + (weight_2 * weight_1 * update + gain_2 * residual)
        out[row] = value.astype(BF16)
        return carry

    lax.fori_loop(0, rows, multiply, 0)


def second_product(cols, near, coarse, low, own, high, product, below, above, peaks):
    rows, blocks, width, _ = coarse.shape
    columns = own.shape[2]
    vmem = pl.BlockSpec(memory_space=VMEM)
    return pl.pallas_call(
        functools.partial(second_kernel, blocks),
        out_shape=jax.ShapeDtypeStruct(own.shape, BF16),
        grid_spec=pltpu.PrefetchScalarGridSpec(
            num_scalar_prefetch=2,
            in_specs=[vmem] * 8,
            out_specs=vmem,
            scratch_shapes=[VMEM((3 * rows, width, columns), BF16)],
        ),
        cost_estimate=pl.CostEstimate(
            flops=2 * coarse.size * columns, bytes_accessed=6 * coarse.size, transcendentals=0
        ),
        name="second_product",
    )(cols, near, coarse, low, own, high, product, below, above, peaks)


def exchange(block, axis):
    return lax.all_to_all(block, axis, split_axis=0, concat_axis=0, tiled=True)


def both_ways(block, axis):
    count = lax.axis_size(axis)
    forward = [(i, i + 1) for i in range(count - 1)]
    backward = [(i + 1, i) for i in range(count - 1)]
    return lax.ppermute(block, axis, forward), lax.ppermute(block, axis, backward)


def routes(fine_agg, balance, coarse_rows):
    group = lax.axis_size("gy")
    me = lax.axis_index("gy")
    rows = fine_agg.shape[0]
    facts = jnp.concatenate([fine_agg, balance.reshape(-1)])
    facts = exchange(jnp.broadcast_to(facts[None], (group,) + facts.shape), "gy")
    named, table = facts[:, :rows], facts[:, rows:].reshape(-1)
    keys = jnp.arange(table.shape[0], dtype=jnp.int32)
    target = jnp.sum(
        jnp.where(named[:, :, None] == keys[None, None, :], table[None, None, :], 0), axis=2
    )
    device = target // coarse_rows
    before = jnp.arange(rows)[:, None] > jnp.arange(rows)[None, :]
    rank = jnp.sum(
        ((device[:, :, None] == device[:, None, :]) & before[None]).astype(jnp.int32), axis=2
    )
    mine = (jnp.arange(group) == me)[:, None]
    place = jnp.sum(jnp.where(mine, device * OCAP + rank, 0), axis=0)
    slots = jnp.arange(group * OCAP, dtype=jnp.int32)
    order = jnp.sum(
        jnp.where(place[None, :] == slots[:, None], jnp.arange(rows, dtype=jnp.int32)[None, :], 0),
        axis=1,
    )
    goal = me * coarse_rows + jnp.arange(coarse_rows, dtype=jnp.int32)
    hit = target[None] == goal[:, None, None]
    slot = jnp.arange(group, dtype=jnp.int32)[:, None] * OCAP + rank
    source = jnp.sum(jnp.where(hit, slot[None] + 1, 0), axis=2)
    found = (source > 0).astype(jnp.int32)
    earlier = jnp.arange(group)[:, None] < jnp.arange(group)[None, :]
    ordinal = jnp.sum(found[:, :, None] * earlier[None].astype(jnp.int32), axis=1)
    members = jnp.stack(
        [
            jnp.sum(jnp.where((ordinal == m) & (found > 0), source - 1, 0), axis=1)
            for m in range(MEMBERS)
        ],
        axis=1,
    )
    return order.astype(jnp.int32), members.astype(jnp.int32)


def per_device(a_blocks, prolong, neighbour, ghost_send, fine_agg, balance, coarse_cols, loads):
    block_rows, blocks = a_blocks.shape[:2]
    group = lax.axis_size("gy")
    row_gy = lax.axis_index("gy")
    row_gx = lax.axis_index("gx")
    devices = group * lax.axis_size("gx")
    coarse_rows = loads.shape[0]
    width = prolong.shape[2]

    low, high = both_ways(loads, "gy")
    outgoing = prolong[ghost_send.reshape(-1)]
    arrived = exchange(outgoing, "gy")
    order, members = routes(fine_agg, balance, coarse_rows)
    columns = jnp.concatenate(
        [jnp.arange(block_rows, dtype=jnp.int32)[:, None], neighbour], axis=1
    )
    parts = chunks_of(blocks)
    received = []
    for first, count in parts:
        sent = galerkin(
            a_blocks, prolong, None if first == 0 else arrived, order, columns, first, count
        )
        received.append(exchange(sent, "gy"))
    so_far = None
    for (first, count), recv in zip(parts[:-1], received[:-1]):
        so_far = gather_rows(
            members, recv, so_far, (coarse_rows, blocks, width, width), first, count
        )
    first_col = (row_gx * group + row_gy - 1) * coarse_rows
    local_cols = coarse_cols - first_col
    coarse, product, sent, peak = first_product(
        members, local_cols, received[-1], so_far, low, loads, high, *parts[-1], devices
    )
    below, above = both_ways(sent, "gy")
    peaks = exchange(peak, ("gx", "gy"))
    here = row_gx * group + row_gy
    near = jnp.stack([jnp.maximum(here - 1, 0), here, jnp.minimum(here + 1, devices - 1)])
    smoothed = second_product(
        local_cols, near.astype(jnp.int32), coarse, low, loads, high, product, below, above, peaks
    )
    return coarse, smoothed


def solution(mesh):
    return jax.shard_map(
        per_device,
        mesh=mesh,
        in_specs=(
            P(("gx", "gy"), None, None, None),
            P(("gx", "gy"), None, None),
            P(("gx", "gy"), None),
            P("gx", "gy", None, None),
            P(("gx", "gy")),
            P("gx", "gy", None),
            P(("gx", "gy"), None),
            P(("gx", "gy"), None, None),
        ),
        out_specs=(P(("gx", "gy"), None, None, None), P(("gx", "gy"), None, None)),
        check_vma=False,
    )
```

time: 417 us -> 258 us (0.62)
  waiting for transfers between devices: 222 us -> 129 us
  Pallas kernels: 0 us -> 59.6 us
  local copies, waits for them, and re-layouts: 59.6 us -> 11.4 us
  blocking collectives: 42.1 us -> 0 us
  matrix products: 36.5 us -> 0 us
  starting transfers between devices: 44.8 us -> 50.4 us
    all_to_all x5 -> x6, waiting for transfers between devices: 184 us -> 79.6 us  [exchange(): return lax.all_to_all(block, axis, split_axis=0, concat_axis=0, tiled=True)]
    pallas_call x0 -> x7, Pallas kernels: none -> 59.6 us  [the longest x3 37.3 us: galerkin(): pl.pallas_call(functools.partial(galerkin_kernel, first, count, per_step,...]
    pmax x1 -> x0, blocking collectives: 42.1 us -> none  [per_device(): largest = lax.pmax(jnp.max(magnitude), ('gx', 'gy'))]
    dot_general x5 -> x0, matrix products: 36.5 us -> none  [the longest x1 19 us: per_device(): jnp.einsum('iac,ikad->ikcd', prolong, applied, preferred_element_type=jnp...]
    scatter x4 -> x0, local copies, waits for them, and re-layouts: 22.6 us -> none  [the longest x2 21.3 us: place_rows(): buffer = jnp.zeros((capacity,) + values.shape[1:], values.dtype).at[posit...]
    gather x4 -> x1, local copies, waits for them, and re-layouts: 16.4 us -> 3.35 us  [per_device(): outgoing = prolong[ghost_send.reshape(-1)]]
    ppermute x4, waiting for transfers between devices: 38.4 us -> 49.8 us  [the longest x2 49.8 us: both_ways(): lax.ppermute(block, axis, forward)]
    convert_element_type x2 -> x0, local copies, waits for them, and re-layouts: 8.74 us -> none  [the longest x1 8.29 us: per_device(): partial_value = jnp.einsum('iac,ikad->ikcd', prolong, applied, preferred_...]
  transfers between devices with their start and end apart: 9 -> 10, of which waited for: 7 -> 5; matrix products, arithmetic and copies ran while one was open for 19% -> 4% of each run, Pallas kernels for 0% -> 17%
where the time goes in v1:
time: 258 us; the launch traced here: 256 us
  waiting for transfers between devices  129 us (50%)
  Pallas kernels  59.6 us (23%)
  starting transfers between devices  50.4 us (20%)
  local copies, waits for them, and re-layouts  11.4 us (4%)
  other arithmetic  4.57 us (2%)
    all_to_all x6, waiting for transfers between devices, exchange(): return lax.all_to_all(block, axis, split_axis=0, concat_axis=0, tiled=True)  79.6 us
    ppermute x2, waiting for transfers between devices, both_ways(): lax.ppermute(block, axis, forward)  49.8 us
    all_to_all x6, starting transfers between devices, exchange(): return lax.all_to_all(block, axis, split_axis=0, concat_axis=0, tiled=True)  38.1 us
    pallas_call x3, Pallas kernels, galerkin(): pl.pallas_call(functools.partial(galerkin_kernel, first, count, per_step,...  37.3 us
    pallas_call x1, Pallas kernels, first_product(): pl.pallas_call(functools.partial(first_kernel, first, count, blocks), out...  8.53 us
    pallas_call x1, Pallas kernels, second_product(): pl.pallas_call(functools.partial(second_kernel, blocks), out_shape=jax.Sh...  7.44 us
    ppermute x2, starting transfers between devices, both_ways(): lax.ppermute(block, axis, backward)  7.35 us
    pallas_call x2, Pallas kernels, gather_rows(): pl.pallas_call(functools.partial(gather_kernel, first, count), out_shape=...  6.33 us
  transfers between devices with their start and end apart: 10, of which 5 were waited for; matrix products, arithmetic and copies ran while one was open for 4% of the time, Pallas kernels for 17%

profile of v1, /device:TPU:17, one launch (start us, length us, event | category | flops | bytes accessed | tf_op | source)
XLA Modules:
  0.0 256.2 jit_solution(11512766295777141346)
XLA Ops:
  0.6 0.7 pad_add_fusion.2
  1.4 0.6 broadcast_in_dim.47
  2.0 5.6 %all-to-all-start = ((s32[8,1,32]{2,1,0:T(1,128)}), s32[8,1,32]{2,1,0:T(1,128)S(1)}, u32[]{:S(2)}, u32[]{:S(2)}) async-start(s32[8,1,32]{2,1,0:T(1,128)} %broadcast_in_dim.47), calls=%async_computation | async-start | bytes 8192 | tf_op jit(solution)/shard_map/all_to_all | solution.py:304
  7.6 0.8 copy.32
  8.3 0.1 reshape.143
  8.4 3.4 %gather_fusion = bf16[24,256,128]{2,1,0:T(8,128)(2,1)} fusion(bf16[24,256,128]{2,1,0:T(8,128)(2,1)} %refs_3_.5, s32[1024]{0:T(1024)S(1)} %pad_clamp_fusion), kind=kCustom, calls=%fused_computation | custom fusion | bytes 3145824 | tf_op jit(solution)/shard_map/gather | solution.py:364
  11.8 5.6 %all-to-all-start.1 = ((bf16[24,256,128]{2,1,0:T(8,128)(2,1)}), bf16[24,256,128]{2,1,0:T(8,128)(2,1)S(1)}, u32[]{:S(2)}, u32[]{:S(2)}) async-start(bf16[24,256,128]{2,1,0:T(8,128)(2,1)} %gather_fusion), calls=%async_computation.1 | async-start | bytes 3145728 | tf_op jit(solution)/shard_map/all_to_all | solution.py:304
  17.4 0.7 copy.33.cols
  18.1 0.1 broadcast_in_dim.52
  18.2 0.3 select_reduce_fusion
  18.5 0.3 convert_reduce_fusion
  18.8 0.1 select_reduce_fusion.3
  18.9 0.6 select_reduce_fusion.2.order
  19.5 10.5 %galerkin_0.1 = bf16[24,1,128,128]{3,2,1,0:T(8,128)(2,1)} custom-call(s32[24]{0:T(128)} %select_reduce_fusion.2.order, s32[24,7]{1,0:T(8,128)} %copy.33.cols, bf16[24,7,256,256]{3,2,1,0:T(8,128)(2,1)} %refs_2_.5, bf16[24,7,256,256]{3,2,1,0:T(8,128)(2,1)} %refs_2_.5, bf16[24,7,256,256]{3,2,1,0:T(8,128)(2,1)} %refs_2_.5, bf16[24,256,128]{2,1,0:T(8,128)(2,1)} %refs_3_.5), custom_call_target="tpu_custom_call" | custom-call | flops 603979776 | bytes 3932160 | tf_op jit(solution)/shard_map/galerkin_0/pallas_call | solution.py:84
  30.1 19.9 %all-to-all-done.1.refs_10_ = bf16[24,256,128]{2,1,0:T(8,128)(2,1)S(1)} async-done(((bf16[24,256,128]{2,1,0:T(8,128)(2,1)}), bf16[24,256,128]{2,1,0:T(8,128)(2,1)S(1)}, u32[]{:S(2)}, u32[]{:S(2)}) %all-to-all-start.1) | async-done | bytes 1572896 | tf_op jit(solution)/shard_map/all_to_all | solution.py:304
  50.0 8.2 %all-to-all-start.4 = ((bf16[24,1,128,128]{3,2,1,0:T(8,128)(2,1)}), bf16[24,1,128,128]{3,2,1,0:T(8,128)(2,1)S(1)}, u32[]{:S(2)}, u32[]{:S(2)}) async-start(bf16[24,1,128,128]{3,2,1,0:T(8,128)(2,1)} %galerkin_0.1), calls=%async_computation.4 | async-start | bytes 1572864 | tf_op jit(solution)/shard_map/all_to_all | solution.py:304
  58.2 13.4 %galerkin_1.1 = bf16[24,3,128,128]{3,2,1,0:T(8,128)(2,1)} custom-call(s32[24]{0:T(128)} %select_reduce_fusion.2.order, s32[24,7]{1,0:T(8,128)} %copy.33.cols, bf16[24,7,256,256]{3,2,1,0:T(8,128)(2,1)} %refs_2_.5, bf16[24,7,256,256]{3,2,1,0:T(8,128)(2,1)} %refs_2_.5, bf16[24,7,256,256]{3,2,1,0:T(8,128)(2,1)} %refs_2_.5, bf16[24,7,256,256]{3,2,1,0:T(8,128)(2,1)} %refs_2_.5, ...), custom_call_target="tpu_custom_call" | custom-call | flops 1811939328 | bytes 11796480 | tf_op jit(solution)/shard_map/galerkin_1/pallas_call | solution.py:84
  71.5 3.9 %all-to-all-done.4.recv = bf16[24,1,128,128]{3,2,1,0:T(8,128)(2,1)S(1)} async-done(((bf16[24,1,128,128]{3,2,1,0:T(8,128)(2,1)}), bf16[24,1,128,128]{3,2,1,0:T(8,128)(2,1)S(1)}, u32[]{:S(2)}, u32[]{:S(2)}) %all-to-all-start.4) | async-done | bytes 786464 | tf_op jit(solution)/shard_map/all_to_all | solution.py:304
  75.4 0.9 copy-done.3
  76.3 6.6 %all-to-all-start.3 = ((bf16[24,3,128,128]{3,2,1,0:T(8,128)(2,1)}), bf16[24,3,128,128]{3,2,1,0:T(8,128)(2,1)S(1)}, u32[]{:S(2)}, u32[]{:S(2)}) async-start(bf16[24,3,128,128]{3,2,1,0:T(8,128)(2,1)} %galerkin_1.1), calls=%async_computation.3 | async-start | bytes 4718592 | tf_op jit(solution)/shard_map/all_to_all | solution.py:304
  83.0 13.4 %galerkin_4.1 = bf16[24,3,128,128]{3,2,1,0:T(8,128)(2,1)} custom-call(s32[24]{0:T(128)} %select_reduce_fusion.2.order, s32[24,7]{1,0:T(8,128)} %copy.33.cols, bf16[24,7,256,256]{3,2,1,0:T(8,128)(2,1)} %refs_2_.5, bf16[24,7,256,256]{3,2,1,0:T(8,128)(2,1)} %refs_2_.5, bf16[24,7,256,256]{3,2,1,0:T(8,128)(2,1)} %refs_2_.5, bf16[24,7,256,256]{3,2,1,0:T(8,128)(2,1)} %refs_2_.5, ...), custom_call_target="tpu_custom_call" | custom-call | flops 1811939328 | bytes 11796480 | tf_op jit(solution)/shard_map/galerkin_4/pallas_call | solution.py:84
  96.4 36.9 %all-to-all-done.3.recv = bf16[24,3,128,128]{3,2,1,0:T(8,128)(2,1)S(1)} async-done(((bf16[24,3,128,128]{3,2,1,0:T(8,128)(2,1)}), bf16[24,3,128,128]{3,2,1,0:T(8,128)(2,1)S(1)}, u32[]{:S(2)}, u32[]{:S(2)}) %all-to-all-start.3) | async-done | bytes 2359328 | tf_op jit(solution)/shard_map/all_to_all | solution.py:304
  133.2 1.4 copy-done.2
  134.6 7.4 %all-to-all-start.2 = ((bf16[24,3,128,128]{3,2,1,0:T(8,128)(2,1)}), bf16[24,3,128,128]{3,2,1,0:T(8,128)(2,1)S(1)}, u32[]{:S(2)}, u32[]{:S(2)}) async-start(bf16[24,3,128,128]{3,2,1,0:T(8,128)(2,1)} %galerkin_4.1), calls=%async_computation.2 | async-start | bytes 4718592 | tf_op jit(solution)/shard_map/all_to_all | solution.py:304
  142.1 3.1 %collective-permute-start = (bf16[8,128,256]{2,1,0:T(8,128)(2,1)S(1)}, bf16[8,128,256]{2,1,0:T(8,128)(2,1)S(1)}, u32[]{:S(2)}, u32[]{:S(2)}) collective-permute-start(bf16[8,128,256]{2,1,0:T(8,128)(2,1)S(1)} %copy-done.4), channel_id=1, source_target_pairs={{0,1},{1,2},{2,3},{3,4},{4,5},{5,6},{6,7},{8,9},{9,10},{10,11},{11... | collective-permute-start | bytes 1572872 | tf_op jit(solution)/shard_map/ppermute | solution.py:311
  145.2 3.1 %collective-permute-start.1 = (bf16[8,128,256]{2,1,0:T(8,128)(2,1)S(1)}, bf16[8,128,256]{2,1,0:T(8,128)(2,1)}, u32[]{:S(2)}, u32[]{:S(2)}) collective-permute-start(bf16[8,128,256]{2,1,0:T(8,128)(2,1)S(1)} %copy-done.4), channel_id=1, source_target_pairs={{1,0},{2,1},{3,2},{4,3},{5,4},{6,5},{7,6},{9,8},{10,9},{11,10},{12... | collective-permute-start | bytes 1572872 | tf_op jit(solution)/shard_map/ppermute | solution.py:311
  148.3 0.6 broadcast_subtract_fusion.cols
  148.9 0.3 select_reduce_fusion.1
  149.2 0.1 multiply_reduce_fusion
  149.3 0.1 select_reduce_fusion.6
  149.4 0.1 copy.29
  149.5 0.1 copy.30
  149.7 0.7 pad_add_fusion.members
  150.3 2.7 %gather_0.1.refs_0_ = bf16[8,7,128,128]{3,2,1,0:T(8,128)(2,1)} custom-call(s32[8,3]{1,0:T(8,128)} %pad_add_fusion.members, bf16[24,1,128,128]{3,2,1,0:T(8,128)(2,1)} %copy-done.3), custom_call_target="tpu_custom_call" | custom-call | flops 786432 | bytes 1179648 | tf_op jit(solution)/shard_map/gather_0/pallas_call | solution.py:129
  153.1 3.6 %gather_1.1.so_far = bf16[8,7,128,128]{3,2,1,0:T(8,128)(2,1)} custom-call(s32[8,3]{1,0:T(8,128)} %pad_add_fusion.members, bf16[24,3,128,128]{3,2,1,0:T(8,128)(2,1)} %copy-done.2, bf16[8,7,128,128]{3,2,1,0:T(8,128)(2,1)} %gather_0.1.refs_0_), custom_call_target="tpu_custom_call", output_to_operand_aliasing={{}: (2, {})} | custom-call | flops 2359296 | bytes 3538944 | tf_op jit(solution)/shard_map/gather_1/pallas_call | solution.py:129
  156.7 49.8 %collective-permute-done.low = bf16[8,128,256]{2,1,0:T(8,128)(2,1)S(1)} collective-permute-done((bf16[8,128,256]{2,1,0:T(8,128)(2,1)S(1)}, bf16[8,128,256]{2,1,0:T(8,128)(2,1)S(1)}, u32[]{:S(2)}, u32[]{:S(2)}) %collective-permute-start) | collective-permute-done | bytes 524320 | tf_op jit(solution)/shard_map/ppermute | solution.py:311
  206.5 0.8 copy-done.5
  207.3 1.4 copy-done.1
  208.7 8.5 %first_product.1 = (bf16[8,7,128,128]{3,2,1,0:T(8,128)(2,1)}, f32[8,128,256]{2,1,0:T(8,128)}, bf16[8,128,256]{2,1,0:T(8,128)(2,1)}, f32[32,8,128]{2,1,0:T(8,128)}) custom-call(s32[8,3]{1,0:T(8,128)} %pad_add_fusion.members, s32[8,7]{1,0:T(8,128)} %broadcast_subtract_fusion.cols, ...), custom_call_target="tpu_custom_call", output_to_operand_aliasing={{0}: (3, {})} | custom-call | flops 469762048 | bytes 5505024 | tf_op jit(solution)/shard_map/first_product/pallas_call | solution.py:214
  217.2 1.9 collective-permute-start.2
  219.2 4.3 %collective-permute-start.3 = (bf16[8,128,256]{2,1,0:T(8,128)(2,1)}, bf16[8,128,256]{2,1,0:T(8,128)(2,1)S(1)}, u32[]{:S(2)}, u32[]{:S(2)}) collective-permute-start(bf16[8,128,256]{2,1,0:T(8,128)(2,1)} %get-tuple-element.8), channel_id=1, source_target_pairs={{1,0},{2,1},{3,2},{4,3},{5,4},{6,5},{7,6},{9,8},{10,9},{11,10},{12... | collective-permute-start | bytes 1572872 | tf_op jit(solution)/shard_map/ppermute | solution.py:311
  223.4 4.7 %all-to-all-start.5 = ((f32[32,8,128]{2,1,0:T(8,128)}), f32[32,8,128]{2,1,0:T(8,128)S(1)}, u32[]{:S(2)}, u32[]{:S(2)}) async-start(f32[32,8,128]{2,1,0:T(8,128)} %get-tuple-element.9), calls=%async_computation.5 | async-start | bytes 262144 | tf_op jit(solution)/shard_map/all_to_all | solution.py:304
  228.1 0.7 pad_add_fusion.3.near
  228.8 18.9 %all-to-all-done.5.peaks = f32[32,8,128]{2,1,0:T(8,128)S(1)} async-done(((f32[32,8,128]{2,1,0:T(8,128)}), f32[32,8,128]{2,1,0:T(8,128)S(1)}, u32[]{:S(2)}, u32[]{:S(2)}) %all-to-all-start.5) | async-done | bytes 131104 | tf_op jit(solution)/shard_map/all_to_all | solution.py:304
  247.7 0.6 copy-done.6
  248.4 0.2 copy-done.7
  248.6 0.2 copy-done.8
  248.7 7.4 %second_product.1 = bf16[8,128,256]{2,1,0:T(8,128)(2,1)} custom-call(s32[8,7]{1,0:T(8,128)} %broadcast_subtract_fusion.cols, s32[3]{0:T(128)} %pad_add_fusion.3.near, bf16[8,7,128,128]{3,2,1,0:T(8,128)(2,1)} %get-tuple-element.4.coarse, bf16[8,128,256]{2,1,0:T(8,128)(2,1)} %copy-done.5, bf16[8,128,256]{2,1,0:T(8,128)(2,1)} %own.3, ...), custom_call_target="tpu_custom_call" | custom-call | flops 469762048 | bytes 5505024 | tf_op jit(solution)/shard_map/second_product/pallas_call | solution.py:287
  (32 shorter events, 0.3 us)
Async XLA Ops:
  2.0 9.8 %all-to-all-start = ((s32[8,1,32]{2,1,0:T(1,128)}), s32[8,1,32]{2,1,0:T(1,128)S(1)}, u32[]{:S(2)}, u32[]{:S(2)}) async-start(s32[8,1,32]{2,1,0:T(1,128)} %broadcast_in_dim.47), calls=%async_computation | async-start | bytes 8192 | tf_op jit(solution)/shard_map/all_to_all | solution.py:304
  11.8 5.6 %copy-start.9 = (s32[24,6]{0,1:T(8,128)S(1)}, s32[24,6]{0,1:T(8,128)}, u32[]{:S(2)}) copy-start(s32[24,6]{0,1:T(8,128)} %param.10) | copy-start | bytes 1732
  11.8 38.2 %all-to-all-start.1 = ((bf16[24,256,128]{2,1,0:T(8,128)(2,1)}), bf16[24,256,128]{2,1,0:T(8,128)(2,1)S(1)}, u32[]{:S(2)}, u32[]{:S(2)}) async-start(bf16[24,256,128]{2,1,0:T(8,128)(2,1)} %gather_fusion), calls=%async_computation.1 | async-start | bytes 3145728 | tf_op jit(solution)/shard_map/all_to_all | solution.py:304
  50.0 8.2 %copy-start = (bf16[24,256,128]{2,1,0:T(8,128)(2,1)}, bf16[24,256,128]{2,1,0:T(8,128)(2,1)S(1)}, u32[]{:S(2)}) copy-start(bf16[24,256,128]{2,1,0:T(8,128)(2,1)S(1)} %all-to-all-done.1.refs_10_) | copy-start | bytes 4718596
  50.0 25.5 %all-to-all-start.4 = ((bf16[24,1,128,128]{3,2,1,0:T(8,128)(2,1)}), bf16[24,1,128,128]{3,2,1,0:T(8,128)(2,1)S(1)}, u32[]{:S(2)}, u32[]{:S(2)}) async-start(bf16[24,1,128,128]{3,2,1,0:T(8,128)(2,1)} %galerkin_0.1), calls=%async_computation.4 | async-start | bytes 1572864 | tf_op jit(solution)/shard_map/all_to_all | solution.py:304
  75.4 0.9 copy-start.3
  76.3 56.9 %all-to-all-start.3 = ((bf16[24,3,128,128]{3,2,1,0:T(8,128)(2,1)}), bf16[24,3,128,128]{3,2,1,0:T(8,128)(2,1)S(1)}, u32[]{:S(2)}, u32[]{:S(2)}) async-start(bf16[24,3,128,128]{3,2,1,0:T(8,128)(2,1)} %galerkin_1.1), calls=%async_computation.3 | async-start | bytes 4718592 | tf_op jit(solution)/shard_map/all_to_all | solution.py:304
  96.4 45.7 %copy-start.4 = (bf16[8,128,256]{2,1,0:T(8,128)(2,1)S(1)}, bf16[8,128,256]{2,1,0:T(8,128)(2,1)}, u32[]{:S(2)}) copy-start(bf16[8,128,256]{2,1,0:T(8,128)(2,1)} %own.3) | copy-start | bytes 1572868
  96.4 51.9 %copy-start.10 = (s32[8,7]{1,0:T(8,128)S(1)}, s32[8,7]{1,0:T(8,128)}, u32[]{:S(2)}) copy-start(s32[8,7]{1,0:T(8,128)} %param.14) | copy-start | bytes 676
  133.2 1.4 copy-start.2
  134.6 71.9 %all-to-all-start.2 = ((bf16[24,3,128,128]{3,2,1,0:T(8,128)(2,1)}), bf16[24,3,128,128]{3,2,1,0:T(8,128)(2,1)S(1)}, u32[]{:S(2)}, u32[]{:S(2)}) async-start(bf16[24,3,128,128]{3,2,1,0:T(8,128)(2,1)} %galerkin_4.1), calls=%async_computation.2 | async-start | bytes 4718592 | tf_op jit(solution)/shard_map/all_to_all | solution.py:304
  142.1 64.4 %collective-permute-start = (bf16[8,128,256]{2,1,0:T(8,128)(2,1)S(1)}, bf16[8,128,256]{2,1,0:T(8,128)(2,1)S(1)}, u32[]{:S(2)}, u32[]{:S(2)}) collective-permute-start(bf16[8,128,256]{2,1,0:T(8,128)(2,1)S(1)} %copy-done.4), channel_id=1, source_target_pairs={{0,1},{1,2},{2,3},{3,4},{4,5},{5,6},{6,7},{8,9},{9,10},{10,11},{11... | collective-permute-start | bytes 1572872 | tf_op jit(solution)/shard_map/ppermute | solution.py:311
  145.2 61.3 %collective-permute-start.1 = (bf16[8,128,256]{2,1,0:T(8,128)(2,1)S(1)}, bf16[8,128,256]{2,1,0:T(8,128)(2,1)}, u32[]{:S(2)}, u32[]{:S(2)}) collective-permute-start(bf16[8,128,256]{2,1,0:T(8,128)(2,1)S(1)} %copy-done.4), channel_id=1, source_target_pairs={{1,0},{2,1},{3,2},{4,3},{5,4},{6,5},{7,6},{9,8},{10,9},{11,10},{12... | collective-permute-start | bytes 1572872 | tf_op jit(solution)/shard_map/ppermute | solution.py:311
  206.5 0.8 copy-start.5
  207.3 1.4 copy-start.1
  217.2 30.5 %collective-permute-start.2 = (bf16[8,128,256]{2,1,0:T(8,128)(2,1)}, bf16[8,128,256]{2,1,0:T(8,128)(2,1)S(1)}, u32[]{:S(2)}, u32[]{:S(2)}) collective-permute-start(bf16[8,128,256]{2,1,0:T(8,128)(2,1)} %get-tuple-element.8), channel_id=1, source_target_pairs={{0,1},{1,2},{2,3},{3,4},{4,5},{5,6},{6,7},{8,9},{9,10},{10,11},{11... | collective-permute-start | bytes 1572872 | tf_op jit(solution)/shard_map/ppermute | solution.py:311
  219.2 28.5 %collective-permute-start.3 = (bf16[8,128,256]{2,1,0:T(8,128)(2,1)}, bf16[8,128,256]{2,1,0:T(8,128)(2,1)S(1)}, u32[]{:S(2)}, u32[]{:S(2)}) collective-permute-start(bf16[8,128,256]{2,1,0:T(8,128)(2,1)} %get-tuple-element.8), channel_id=1, source_target_pairs={{1,0},{2,1},{3,2},{4,3},{5,4},{6,5},{7,6},{9,8},{10,9},{11,10},{12... | collective-permute-start | bytes 1572872 | tf_op jit(solution)/shard_map/ppermute | solution.py:311
  223.4 24.3 %all-to-all-start.5 = ((f32[32,8,128]{2,1,0:T(8,128)}), f32[32,8,128]{2,1,0:T(8,128)S(1)}, u32[]{:S(2)}, u32[]{:S(2)}) async-start(f32[32,8,128]{2,1,0:T(8,128)} %get-tuple-element.9), calls=%async_computation.5 | async-start | bytes 262144 | tf_op jit(solution)/shard_map/all_to_all | solution.py:304
  247.7 0.7 copy-start.6
  247.7 0.9 copy-start.7
  247.7 1.0 copy-start.8
